TPU v7x, 32 devices: a whole 2x2x4 slice. The times are simulated.
32 devices in a mesh: grp: 2 (over y), blk: 4 (over z), tile: 4 (over x, core).
Axes of the slice: x: 2, y: 2, z: 4, core: 2. Of those that a mesh axis runs over, the one named last changes fastest.
Arguments:
- fp_values: bfloat16 [6144, 128], P(('grp', 'blk', 'tile')), parts along dimension 0, may hold values from -0.625 to 0.625
- block_owner: int32 [6144], P(('grp', 'blk', 'tile')), parts along dimension 0, may hold values from 0 to 3, as said below
- block_obs: int32 [6144], P(('grp', 'blk', 'tile')), parts along dimension 0, may hold values from 0 to 127
- block_base: int32 [6144], P(('grp', 'blk', 'tile')), parts along dimension 0, may hold values from 0 to 64
- block_count: int32 [6144], P(('grp', 'blk', 'tile')), parts along dimension 0, may hold values from 32 to 128, as said below
- cover_index: int32 [2, 128], replicated, may hold values from 0 to 191
- cover_weight: float32 [2, 128], replicated, may hold values from 0.25 to 1
- spatial_cov: bfloat16 [2048, 1024], P(('grp', 'blk'), 'tile'), parts along dimension 0, as said below
- temporal_cov: float32 [104, 52], P('grp'), parts along dimension 0, as said below
- obs_week: int32 [1024], P('grp'), parts along dimension 0, may hold values from 0 to 51
- obs_error: float32 [1024], P(('grp', 'blk')), parts along dimension 0, may hold values from 0.2 to 1
Outputs:
- panel: float32 [1024, 128], P(('grp', 'blk')), parts along dimension 0
- trailing: float32 [1024, 512], P(('grp', 'blk'), 'tile'), parts along dimension 0
There are 2 independent parts, one for each index of `grp`. A program takes and returns all parts, laid end to end along the dimension named above; an argument that names none is the same for every part. Nothing has to cross between parts.
Inputs may be any that keep to these rules, and one draw needn't show every extreme that they name: `block_owner`: no tile is named by more than 64 of one device's 192 blocks; in every observation block one tile is named by exactly 64 blocks of each of its devices. `block_count`: each device holds at least one block with all cells valid. `spatial_cov`: symmetric positive definite. `temporal_cov`: symmetric positive definite.
All inputs are finite; a program needn't handle non-finite values.
Results may differ from a plain program's by a relative error of at most 0.0033.
Values may be sent and summed in bfloat16 or wider, within the bound.
No kernel may reach another device: no remote copies, remote signals or barrier semaphores. Data moves between devices by JAX's collectives and lax.ppermute only.
A program may use at most 64 MiB of HBM per device.

v0:
```python
import jax
import jax.numpy as jnp
from jax import lax
from jax.sharding import PartitionSpec as P

PANEL_MAX = 128


def broadcast(value, axis, root):
    mine = lax.axis_index(axis) == root
    return lax.psum(jnp.where(mine, value, jnp.zeros_like(value)), axis)


def kept_values(fp_values, block_count):
    keep_mask = lax.broadcasted_iota(jnp.int32, fp_values.shape, 1) < block_count[:, None]
    return jnp.where(keep_mask, fp_values, jnp.zeros_like(fp_values))


def regrid(values, rows, offsets, cover_index, cover_weight, out_rows, out_cols):
    contrib = values.astype(jnp.float32)[:, None, :] * cover_weight[None, :, :]
    columns = offsets[:, None, None] + cover_index[None, :, :]
    row_index = jnp.broadcast_to(rows[:, None, None], columns.shape)
    return jnp.zeros((out_rows, out_cols), jnp.float32).at[row_index, columns].add(contrib)


def top_rows(local, rank):
    return jnp.where(rank == 0, local, jnp.zeros_like(local))


def contract_last(left, right):
    return lax.dot_general(
        left, right, (((1,), (1,)), ((), ())), preferred_element_type=jnp.float32
    )


def body(
    fp_values,
    block_owner,
    block_obs,
    block_base,
    block_count,
    cover_index,
    cover_weight,
    spatial_cov,
    temporal_cov,
    obs_week,
    obs_error,
):
    n_tile = lax.axis_size("tile")
    n_blk = lax.axis_size("blk")
    tile_rank = lax.axis_index("tile")
    blk_rank = lax.axis_index("blk")
    cell_tile = spatial_cov.shape[1]
    obs_rows = obs_error.shape[0]
    all_cells = cell_tile * n_tile
    col_count = obs_rows * n_blk // n_tile
    panel_width = min(PANEL_MAX, col_count)
    kept = kept_values(fp_values, block_count)
    dense = regrid(
        kept,
        block_obs,
        block_owner * cell_tile + block_base,
        cover_index,
        cover_weight,
        obs_rows,
        all_cells,
    )
    tile_sum = lax.psum_scatter(dense, "tile", scatter_dimension=1, tiled=True)
    footprints = tile_sum.astype(jnp.bfloat16)
    row_prints = lax.all_gather(footprints, "tile", axis=1, tiled=True)
    product = jnp.dot(
        row_prints,
        lax.all_gather(spatial_cov, "blk", axis=0, tiled=True),
        preferred_element_type=jnp.float32,
    ).astype(jnp.bfloat16)
    terms = contract_last(product, lax.all_gather(footprints, "blk", axis=0, tiled=True))
    pairs = lax.psum_scatter(terms, "tile", scatter_dimension=1, tiled=True)
    week_count = temporal_cov.shape[0]
    week_ids = jnp.arange(week_count, dtype=jnp.int32)
    row_weeks = lax.dynamic_slice_in_dim(obs_week, blk_rank * obs_rows, obs_rows)
    col_weeks = lax.dynamic_slice_in_dim(obs_week, tile_rank * col_count, col_count)
    row_onehot = (row_weeks[:, None] == week_ids[None, :]).astype(jnp.float32)
    col_onehot = (col_weeks[:, None] == week_ids[None, :]).astype(jnp.float32)
    row_cov = jnp.dot(row_onehot, temporal_cov, precision=lax.Precision.HIGHEST)
    week_cov = lax.dot_general(
        row_cov, col_onehot, (((1,), (1,)), ((), ())), precision=lax.Precision.HIGHEST
    )
    row_global = blk_rank * obs_rows + jnp.arange(obs_rows, dtype=jnp.int32)
    col_global = tile_rank * col_count + jnp.arange(col_count, dtype=jnp.int32)
    diagonal = jnp.where(row_global[:, None] == col_global[None, :], obs_error[:, None], 0.0)
    innovation = pairs * week_cov + diagonal
    panel_columns = broadcast(innovation[:, :panel_width], "tile", 0)
    top_group, top_left = lax.psum(
        (top_rows(innovation, blk_rank), top_rows(panel_columns, blk_rank)), "blk"
    )
    pivot = jnp.linalg.cholesky(0.5 * (top_left + top_left.T))
    panel = jax.scipy.linalg.solve_triangular(pivot, panel_columns.T, lower=True).T
    column_factor = jax.scipy.linalg.solve_triangular(pivot, top_group, lower=True).T
    trailing = innovation - jnp.dot(panel, column_factor.T, precision=lax.Precision.HIGHEST)
    return (panel, trailing)


def solution(mesh):
    placed = (
        P(("grp", "blk", "tile"), None),
        P(("grp", "blk", "tile")),
        P(("grp", "blk", "tile")),
        P(("grp", "blk", "tile")),
        P(("grp", "blk", "tile")),
        P(),
        P(),
        P(("grp", "blk"), "tile"),
        P("grp", None),
        P("grp"),
        P(("grp", "blk")),
    )
    return jax.shard_map(
        body,
        mesh=mesh,
        in_specs=placed,
        out_specs=(P(("grp", "blk"), None), P(("grp", "blk"), "tile")),
        check_vma=False,
    )
```

profile of v0, /device:TPU:0, one launch (start us, length us, event | category | flops | bytes accessed | tf_op | source)
XLA Modules:
  0.0 524.8 jit_solution(15512923887324170173)
XLA Ops:
  7.2 0.7 broadcast_add_fusion
  8.0 0.7 copy-done.10
  8.6 0.7 copy-done.7
  9.5 0.6 copy-done.14
  10.3 0.5 copy-done.15
  11.1 0.6 copy-done.5
  11.8 0.6 copy-done.9
  12.5 339.3 %scatter_custom_fusion = f32[131072]{0:T(1024)S(1)} fusion(s32[49152]{0:T(1024)S(1)} %bitcast.32, f32[49152]{0:T(1024)S(1)} %bitcast.33, f32[]{:T(128)} %constant.58.clone.1), kind=kCustom, calls=%fused_computation.10 | custom fusion | flops 49152 | bytes 524292
  351.8 0.9 reshape.48
  352.8 0.8 copy-done.3
  353.6 17.4 %all_gather.10 = bf16[1024,256]{1,0:T(8,128)(2,1)S(1)} all-gather(bf16[256,256]{1,0:T(8,128)(2,1)S(1)} %copy-done.3), channel_id=1, replica_groups=mesh['grp'=2,'blk'=4,'tile'=4] {'blk'}, dimensions={0}, use_global_device_ids=true | all-gather | bytes 655360 | tf_op jit(solution)/shard_map/all_gather | solution.py:73
  371.0 6.3 %reduce-scatter.3.cloned.1.call-done = f32[128,256]{1,0:T(8,128)} async-done(((f32[128,1024]{1,0:T(8,128)}), f32[128,256]{1,0:T(8,128)}) %reduce-scatter.3.cloned.1.call-update) | async-done | bytes 131088 | tf_op jit(solution)/shard_map/reduce_scatter | solution.py:68
  377.3 0.9 convert_element_type.12
  378.2 13.8 %all_gather.11 = bf16[512,256]{1,0:T(8,128)(2,1)S(1)} all-gather(bf16[128,256]{1,0:T(8,128)(2,1)S(1)} %convert_element_type.12), channel_id=1, replica_groups=mesh['grp'=2,'blk'=4,'tile'=4] {'blk'}, dimensions={0}, use_global_device_ids=true | all-gather | bytes 327680 | tf_op jit(solution)/shard_map/all_gather | solution.py:76
  392.0 5.8 %all_gather.9 = bf16[128,1024]{1,0:T(8,128)(2,1)S(1)} all-gather(bf16[128,256]{1,0:T(8,128)(2,1)S(1)} %convert_element_type.12), channel_id=1, replica_groups=mesh['grp'=2,'blk'=4,'tile'=4] {'tile'}, dimensions={1}, use_global_device_ids=true | all-gather | bytes 327680 | tf_op jit(solution)/shard_map/all_gather | solution.py:70
  397.7 1.2 fusion
  399.0 0.7 copy-done.13
  400.1 19.8 %reduce-scatter.5.cloned.1.call-done = f32[128,128]{1,0:T(8,128)} async-done(((f32[128,512]{1,0:T(8,128)}), f32[128,128]{1,0:T(8,128)}) %reduce-scatter.5.cloned.1.call-update) | async-done | bytes 65552 | tf_op jit(solution)/shard_map/reduce_scatter | solution.py:77
  419.9 0.7 copy-done.12
  420.5 1.8 broadcast_select_fusion.2
  422.4 31.9 %all-reduce.4.cloned.1.call-done = f32[128,128]{1,0:T(8,128)} async-done(((f32[128,128]{1,0:T(8,128)}), f32[128,128]{1,0:T(8,128)}) %all-reduce.4.cloned.1.call-update) | async-done | bytes 65552 | tf_op jit(solution)/shard_map/psum | solution.py:11
  454.3 1.5 broadcast_select_fusion.3
  455.8 36.0 %all-reduce.6.cloned.1.call-done = (f32[128,128]{1,0:T(8,128)}, f32[128,128]{1,0:T(8,128)}) async-done(((f32[128,128]{1,0:T(8,128)}, f32[128,128]{1,0:T(8,128)}), (f32[128,128]{1,0:T(8,128)}, f32[128,128]{1,0:T(8,128)})) %all-reduce.6.cloned.1.call-update) | async-done | bytes 131088 | tf_op jit(solution)/shard_map/psum | solution.py:93
  491.8 1.0 copy.23
  493.0 11.7 %cholesky.17 = f32[128,128]{1,0:T(8,128)S(1)} custom-call(f32[128,128]{1,0:T(8,128)S(1)} %fusion.11), custom_call_target="Cholesky" | custom-call | tf_op jit(solution)/shard_map/jit(cholesky)/cholesky | solution.py:96
  504.7 0.6 compare_reduce_fusion
  505.4 0.7 fusion.5
  506.1 9.8 %custom-call.7 = f32[1,128,128]{1,2,0:T(8,128)S(1)} custom-call(f32[1,128,128]{2,1,0:T(8,128)S(1)} %fusion.5), custom_call_target="InvertDiagBlocksLowerTriangular" | custom-call | tf_op jit(solution)/shard_map/jit(_solve_triangular)/triangular_solve | solution.py:97
  515.9 0.3 fusion.6
  516.2 0.7 copy.25
  517.0 0.3 fusion.8
  517.3 0.9 convolution_subtract_fusion
  (47 shorter events, 1.6 us)
Async XLA Ops:
  7.2 392.6 %copy-start = (f32[52,52]{1,0:T(8,128)S(1)}, f32[52,52]{1,0:T(8,128)}, u32[]{:S(2)}) copy-start(f32[52,52]{1,0:T(8,128)} %param.21) | copy-start | bytes 32452
  7.2 0.8 copy-start.6
  7.2 370.1 %reduce-scatter.3.cloned.1.call-start = ((), (), s32[]{:S(2)}) async-start(), calls=%async_computation.2 | async-start | bytes 655360 | tf_op jit(solution)/shard_map/reduce_scatter | solution.py:68
  7.2 0.7 copy-start.11
  7.9 0.7 copy-start.10
  8.6 0.7 copy-start.7
  9.5 0.7 copy-start.14
  10.1 0.7 copy-start.15
  10.9 0.8 copy-start.5
  10.9 0.8 copy-start.8
  11.7 0.7 copy-start.9
  352.7 0.9 copy-start.3
  352.7 67.2 %reduce-scatter.5.cloned.1.call-start = ((), (), s32[]{:S(2)}) async-start(), calls=%async_computation.3 | async-start | bytes 327680 | tf_op jit(solution)/shard_map/reduce_scatter | solution.py:77
  398.9 55.4 %all-reduce.4.cloned.1.call-start = ((), (), s32[]{:S(2)}) async-start(), calls=%async_computation.4 | async-start | bytes 131072 | tf_op jit(solution)/shard_map/psum | solution.py:11
  399.0 0.7 copy-start.13
  419.9 0.7 copy-start.12
  422.3 69.5 %all-reduce.6.cloned.1.call-start = ((), (), s32[]{:S(2)}) async-start(), calls=%async_computation.5 | async-start | bytes 262144 | tf_op jit(solution)/shard_map/psum | solution.py:93
  491.8 1.0 copy-start.2
  505.4 10.5 %copy-start.1 = (f32[128,128]{1,0:T(8,128)S(1)}, f32[128,128]{1,0:T(8,128)}, u32[]{:S(2)}) copy-start(f32[128,128]{1,0:T(8,128)} %all-reduce.4.cloned.1.call-done) | copy-start | bytes 196612
  516.2 0.8 copy-start.4
Sparse Core Ops, SparseCore 0:
  352.8 24.3 reduce-scatter.2
  399.1 20.7 reduce-scatter.4
  422.8 31.5 all-reduce.3
  457.1 34.6 all-reduce.5
where the time goes:
time: 525 us
  other arithmetic  366 us (70%)
  waiting for transfers between devices  94.1 us (18%)
  blocking collectives  36.9 us (7%)
  between operations  14 us (3%)
  local copies, waits for them, and re-layouts  8.9 us (2%)
    unnamed x4, other arithmetic  340 us
    psum x1, waiting for transfers between devices, body(): lax.psum((top_rows(innovation, blk_rank), top_rows(panel_columns, blk_ran...  36 us
    psum x1, waiting for transfers between devices, broadcast(): return lax.psum(jnp.where(mine, value, jnp.zeros_like(value)), axis)  31.9 us
    reduce_scatter x1, waiting for transfers between devices, body(): pairs = lax.psum_scatter(terms, 'tile', scatter_dimension=1, tiled=True)  19.8 us
    all_gather x1, blocking collectives, body(): lax.all_gather(spatial_cov, 'blk', axis=0, tiled=True)  17.4 us
    all_gather x1, blocking collectives, body(): lax.all_gather(footprints, 'blk', axis=0, tiled=True)  13.8 us
    another operation x3, other arithmetic, body(): pivot = jnp.linalg.cholesky(0.5 * (top_left + top_left.T))  12.4 us
  transfers between devices with their start and end apart: 4, of which 4 were waited for; matrix products, arithmetic and copies ran while one was open for 0% of the time, Pallas kernels for 0%

commit v1 on v0

--- a/solution.py
+++ b/solution.py
@@ -6,9 +6,15 @@
 PANEL_MAX = 128
 
 
+def summed_here(x, axis):
+    parts = lax.all_gather(x, axis, axis=0, tiled=False)
+    total = parts.sum(axis=0)
+    return total
+
+
 def broadcast(value, axis, root):
     mine = lax.axis_index(axis) == root
-    return lax.psum(jnp.where(mine, value, jnp.zeros_like(value)), axis)
+    return summed_here(jnp.where(mine, value, jnp.zeros_like(value)), axis)
 
 
 def kept_values(fp_values, block_count):

time: 525 us -> 497 us (0.947)
  waiting for transfers between devices: 94.1 us -> 61 us
  blocking collectives: 36.9 us -> 42.7 us
    psum x1 -> x0, waiting for transfers between devices: 31.9 us -> none  [broadcast(): return lax.psum(jnp.where(mine, value, jnp.zeros_like(value)), axis)]
    all_gather x0 -> x1, blocking collectives: none -> 5.76 us  [summed_here(): parts = lax.all_gather(x, axis, axis=0, tiled=False)]
  transfers between devices with their start and end apart: 4 -> 3, of which waited for: 4 -> 3; matrix products, arithmetic and copies ran while one was open for 0% -> 0% of each run, Pallas kernels for 0% -> 0%
where the time goes in v1:
time: 497 us; the launch traced here: 496 us
  other arithmetic  365 us (73%)
  waiting for transfers between devices  61 us (12%)
  blocking collectives  42.7 us (9%)
  between operations  14 us (3%)
  local copies, waits for them, and re-layouts  8.9 us (2%)
    unnamed x4, other arithmetic  340 us
    psum x1, waiting for transfers between devices, body(): lax.psum((top_rows(innovation, blk_rank), top_rows(panel_columns, blk_ran...  34.9 us
    reduce_scatter x1, waiting for transfers between devices, body(): pairs = lax.psum_scatter(terms, 'tile', scatter_dimension=1, tiled=True)  19.8 us
    all_gather x1, blocking collectives, body(): lax.all_gather(spatial_cov, 'blk', axis=0, tiled=True)  17.4 us
    all_gather x1, blocking collectives, body(): lax.all_gather(footprints, 'blk', axis=0, tiled=True)  13.8 us
    another operation x3, other arithmetic, body(): pivot = jnp.linalg.cholesky(0.5 * (top_left + top_left.T))  12.4 us
    another operation x2, other arithmetic, body(): jax.scipy.linalg.solve_triangular(pivot, panel_columns.T, lower=True)  10.5 us
  transfers between devices with their start and end apart: 3, of which 3 were waited for; matrix products, arithmetic and copies ran while one was open for 0% of the time, Pallas kernels for 0%

profile of v1, /device:TPU:0, one launch (start us, length us, event | category | flops | bytes accessed | tf_op | source)
XLA Modules:
  0.0 496.5 jit_solution(4993028759853959987)
XLA Ops:
  7.2 0.7 broadcast_add_fusion
  8.0 0.7 copy-done.9
  8.6 0.7 copy-done.6
  9.5 0.6 copy-done.13
  10.3 0.5 copy-done.14
  11.1 0.6 copy-done.4
  11.8 0.6 copy-done.8
  12.5 339.3 %scatter_custom_fusion = f32[131072]{0:T(1024)S(1)} fusion(s32[49152]{0:T(1024)S(1)} %bitcast.34, f32[49152]{0:T(1024)S(1)} %bitcast.35, f32[]{:T(128)} %constant.58.clone.1), kind=kCustom, calls=%fused_computation.10 | custom fusion | flops 49152 | bytes 524292
  351.8 0.9 reshape.48
  352.8 0.8 copy-done.2
  353.6 17.4 %all_gather.16 = bf16[1024,256]{1,0:T(8,128)(2,1)S(1)} all-gather(bf16[256,256]{1,0:T(8,128)(2,1)S(1)} %copy-done.2), channel_id=1, replica_groups=mesh['grp'=2,'blk'=4,'tile'=4] {'blk'}, dimensions={0}, use_global_device_ids=true | all-gather | bytes 655360 | tf_op jit(solution)/shard_map/all_gather | solution.py:79
  371.0 6.3 %reduce-scatter.3.cloned.1.call-done = f32[128,256]{1,0:T(8,128)} async-done(((f32[128,1024]{1,0:T(8,128)}), f32[128,256]{1,0:T(8,128)}) %reduce-scatter.3.cloned.1.call-update) | async-done | bytes 131088 | tf_op jit(solution)/shard_map/reduce_scatter | solution.py:74
  377.2 0.9 convert_element_type.12
  378.2 13.8 %all_gather.17 = bf16[512,256]{1,0:T(8,128)(2,1)S(1)} all-gather(bf16[128,256]{1,0:T(8,128)(2,1)S(1)} %convert_element_type.12), channel_id=1, replica_groups=mesh['grp'=2,'blk'=4,'tile'=4] {'blk'}, dimensions={0}, use_global_device_ids=true | all-gather | bytes 327680 | tf_op jit(solution)/shard_map/all_gather | solution.py:82
  392.0 5.8 %all_gather.15 = bf16[128,1024]{1,0:T(8,128)(2,1)S(1)} all-gather(bf16[128,256]{1,0:T(8,128)(2,1)S(1)} %convert_element_type.12), channel_id=1, replica_groups=mesh['grp'=2,'blk'=4,'tile'=4] {'tile'}, dimensions={1}, use_global_device_ids=true | all-gather | bytes 327680 | tf_op jit(solution)/shard_map/all_gather | solution.py:76
  397.7 1.2 fusion
  399.0 0.7 copy-done.12
  400.0 19.8 %reduce-scatter.5.cloned.1.call-done = f32[128,128]{1,0:T(8,128)} async-done(((f32[128,512]{1,0:T(8,128)}), f32[128,128]{1,0:T(8,128)}) %reduce-scatter.5.cloned.1.call-update) | async-done | bytes 65552 | tf_op jit(solution)/shard_map/reduce_scatter | solution.py:83
  419.9 0.7 copy-done.11
  420.5 1.8 broadcast_select_fusion.2
  422.3 5.8 %all-gather = f32[512,128]{1,0:T(8,128)S(1)} all-gather(f32[128,128]{1,0:T(8,128)S(1)} %get-tuple-element.14), channel_id=2, replica_groups=mesh['grp'=2,'blk'=4,'tile'=4] {'tile'}, dimensions={0}, use_global_device_ids=true | all-gather | bytes 327680 | tf_op jit(solution)/shard_map/all_gather | solution.py:10
  428.1 0.6 broadcast_select_fusion.3
  428.7 34.9 %all-reduce.3.cloned.1.call-done = (f32[128,128]{1,0:T(8,128)}, f32[128,128]{1,0:T(8,128)}) async-done(((f32[128,128]{1,0:T(8,128)}, f32[128,128]{1,0:T(8,128)}), (f32[128,128]{1,0:T(8,128)}, f32[128,128]{1,0:T(8,128)})) %all-reduce.3.cloned.1.call-update) | async-done | bytes 131088 | tf_op jit(solution)/shard_map/psum | solution.py:99
  463.6 1.0 copy.23
  464.8 11.7 %cholesky.17 = f32[128,128]{1,0:T(8,128)S(1)} custom-call(f32[128,128]{1,0:T(8,128)S(1)} %fusion.11), custom_call_target="Cholesky" | custom-call | tf_op jit(solution)/shard_map/jit(cholesky)/cholesky | solution.py:102
  476.5 0.6 compare_reduce_fusion
  477.1 0.7 fusion.5
  477.8 9.8 %custom-call.7 = f32[1,128,128]{1,2,0:T(8,128)S(1)} custom-call(f32[1,128,128]{2,1,0:T(8,128)S(1)} %fusion.5), custom_call_target="InvertDiagBlocksLowerTriangular" | custom-call | tf_op jit(solution)/shard_map/jit(_solve_triangular)/triangular_solve | solution.py:103
  487.6 0.3 fusion.6
  487.9 0.7 copy.25
  488.8 0.3 fusion.8
  489.0 0.9 convolution_subtract_fusion
  (44 shorter events, 1.6 us)
Async XLA Ops:
  7.2 392.6 %copy-start = (f32[52,52]{1,0:T(8,128)S(1)}, f32[52,52]{1,0:T(8,128)}, u32[]{:S(2)}) copy-start(f32[52,52]{1,0:T(8,128)} %param.21) | copy-start | bytes 32452
  7.2 0.8 copy-start.5
  7.2 370.1 %reduce-scatter.3.cloned.1.call-start = ((), (), s32[]{:S(2)}) async-start(), calls=%async_computation.2 | async-start | bytes 655360 | tf_op jit(solution)/shard_map/reduce_scatter | solution.py:74
  7.2 0.7 copy-start.10
  7.9 0.7 copy-start.9
  8.6 0.7 copy-start.6
  9.5 0.7 copy-start.13
  10.1 0.7 copy-start.14
  10.9 0.8 copy-start.4
  10.9 0.8 copy-start.7
  11.7 0.7 copy-start.8
  352.7 0.9 copy-start.2
  352.7 67.2 %reduce-scatter.5.cloned.1.call-start = ((), (), s32[]{:S(2)}) async-start(), calls=%async_computation.3 | async-start | bytes 327680 | tf_op jit(solution)/shard_map/reduce_scatter | solution.py:83
  398.9 64.7 %all-reduce.3.cloned.1.call-start = ((), (), s32[]{:S(2)}) async-start(), calls=%async_computation.4 | async-start | bytes 262144 | tf_op jit(solution)/shard_map/psum | solution.py:99
  399.0 0.7 copy-start.12
  419.9 0.7 copy-start.11
  463.6 1.0 copy-start.1
  487.9 0.8 copy-start.3
Sparse Core Ops, SparseCore 0:
  352.8 24.3 reduce-scatter.2
  399.1 20.7 reduce-scatter.4
  428.9 34.6 all-reduce.2
